TPU v7x, 512 devices: a whole 4x4x16 slice. The times are simulated.
512 devices in a mesh: ep: 128 (over z, x, core), tp: 4 (over y).
Axes of the slice: x: 4, y: 4, z: 16, core: 2. Of those that a mesh axis runs over, the one named last changes fastest.
Arguments:
- attn_out: bfloat16 [16384, 1536], P('ep', 'tp'), may hold values from -6 to 6
- residual: bfloat16 [16384, 1536], P('ep'), may hold values from -6 to 6
- w_out: bfloat16 [1536, 1536], P('tp'), may hold values from -0.15625 to 0.15625
- w_router: bfloat16 [1536, 40], replicated, may hold values from -0.25 to 0.25
- expert_ids: int32 [16384, 8], P('ep'), may hold values from 0 to 39, as said below
- slot_expert: int32 [128], replicated, may hold values from 0 to 39, as said below
- w_in: bfloat16 [128, 1536, 2, 512], P('ep', None, None, 'tp')
- w_down: bfloat16 [128, 512, 1536], P('ep', None, 'tp')
- norm_gain: float32 [1536], P('tp'), may hold values from 0.25 to 1.75
Outputs:
- normed: bfloat16 [16384, 1536], P('ep', 'tp')
Inputs may be any that keep to these rules, and one draw needn't show every extreme that they name: `slot_expert`: every expert fills at least one and at most four slots; all slots of one expert hold equal w_in and w_down. `expert_ids`: each row names 8 different experts. Within each aligned block of 128 rows, expert e is named by at most 10 * copies[e] rows, and one expert reaches that bound in every block.
All inputs are finite; a program needn't handle non-finite values.
Results may differ from a plain program's by a relative error of at most 0.0067.
Values may be sent and summed in bfloat16 or wider, within the bound.
No kernel may reach another device: no remote copies, remote signals or barrier semaphores. Data moves between devices by JAX's collectives and lax.ppermute only.
A program may use at most 64 MiB of HBM per device.

v0:
```python
import jax
import jax.numpy as jnp
from jax import lax
from jax.sharding import PartitionSpec as P

E = 40


def route(ids, slot_expert, capacity):
    flat = ids.reshape(-1)
    kinds = jnp.arange(E, dtype=jnp.int32)
    onehot = (flat[:, None] == kinds[None, :]).astype(jnp.int32)
    before = jnp.cumsum(onehot, axis=0) - onehot
    rank = jnp.sum(before * onehot, axis=1)
    slot_hot = (slot_expert[:, None] == kinds[None, :]).astype(jnp.int32)
    copies = jnp.sum(slot_hot, axis=0)
    copy_no = jnp.sum((jnp.cumsum(slot_hot, axis=0) - slot_hot) * slot_hot, axis=1)
    mine = jnp.sum(onehot * copies[None, :], axis=1)
    copy_pick = rank % mine
    place = rank // mine
    match = (slot_expert[None, :] == flat[:, None]) & (copy_no[None, :] == copy_pick[:, None])
    slot_ids = jnp.arange(slot_expert.shape[0], dtype=jnp.int32)
    slot = jnp.sum(jnp.where(match, slot_ids[None, :], 0), axis=1)
    return slot * capacity + place


def per_device(
    attn_out, residual, w_out, w_router, expert_ids, slot_expert, w_in, w_down, norm_gain
):
    rows = residual.shape[0]
    width = residual.shape[1]
    quarter = attn_out.shape[1]
    topk = expert_ids.shape[1]
    slots = slot_expert.shape[0]
    nep = lax.axis_size("ep")
    tp_pos = lax.axis_index("tp")
    slot_dev = slots // nep
    capacity = (rows * topk * 5 // 4 + slots - 1) // slots
    partial_value = jnp.dot(attn_out, w_out, preferred_element_type=jnp.float32)
    proj = lax.psum(partial_value, "tp")
    stream = (residual.astype(jnp.float32) + proj).astype(jnp.bfloat16)
    logits = jnp.dot(stream, w_router, preferred_element_type=jnp.float32)
    picked = jnp.take_along_axis(logits, expert_ids, axis=1)
    weights = jnp.exp(picked)
    gates = weights / jnp.sum(weights, axis=1, keepdims=True)
    dest = route(expert_ids, slot_expert, capacity)
    row_of = jnp.arange(rows * topk, dtype=jnp.int32) // topk
    send = jnp.zeros((slots * capacity, width), jnp.bfloat16).at[dest].set(stream[row_of])
    send = send.reshape(nep, slot_dev, 1, capacity, width)
    gu = jnp.einsum(
        "osnce,segf->osncgf",
        lax.all_to_all(send, "ep", split_axis=0, concat_axis=2, tiled=True),
        w_in,
        preferred_element_type=jnp.float32,
    )
    hidden = (jax.nn.silu(gu[..., 0, :]) * gu[..., 1, :]).astype(jnp.bfloat16)
    summed = jnp.einsum(
        "osncf,sfd->osncd",
        lax.all_gather(hidden, "tp", axis=4, tiled=True),
        w_down,
        preferred_element_type=jnp.float32,
    )
    served = summed.astype(jnp.bfloat16)
    back = lax.all_to_all(served, "ep", split_axis=2, concat_axis=0, tiled=True)
    back = back.reshape(slots * capacity, quarter)
    gathered = back[dest].astype(jnp.float32).reshape(rows, topk, quarter)
    moe = jnp.sum(gates[:, :, None] * gathered, axis=1)
    own = lax.dynamic_slice_in_dim(stream, tp_pos * quarter, quarter, 1).astype(jnp.float32)
    mixed = own + moe
    square = lax.psum(jnp.sum(mixed * mixed, axis=1), "tp")
    scale = lax.rsqrt(square / width + 1e-06)
    return (mixed * scale[:, None] * norm_gain[None, :]).astype(jnp.bfloat16)


def solution(mesh):
    return jax.shard_map(
        per_device,
        mesh=mesh,
        in_specs=(
            P("ep", "tp"),
            P("ep", None),
            P("tp", None),
            P(),
            P("ep", None),
            P(),
            P("ep", None, None, "tp"),
            P("ep", None, "tp"),
            P("tp"),
        ),
        out_specs=P("ep", "tp"),
        check_vma=False,
    )
```

profile of v0, /device:TPU:32, one launch (start us, length us, event | category | flops | bytes accessed | tf_op | source)
XLA Modules:
  0.0 551.4 jit_solution(7083496481394436795)
XLA Ops:
  6.5 1.3 copy-done
  7.8 2.2 fusion.27
  10.0 0.8 copy.57
  11.0 11.3 %reduce-window.6 = s32[40,8,128]{2,1,0:T(8,128)S(1)} reduce-window(s32[40,8,128]{2,1,0:T(8,128)S(1)} %fusion.20, s32[]{:T(128)} %constant.60.clone.1), window={size=1x1x128 pad=0_0x0_0x127_0}, to_apply=%region_4.5 | reduce-window | flops 5201920 | bytes 327684 | tf_op jit(solution)/shard_map/reduce-window
  22.4 0.1 copy.59
  22.7 0.1 broadcast_add_fusion
  22.9 0.2 reduce_window_sum.26
  23.1 0.2 fusion.22
  23.3 0.1 fusion.26
  23.5 0.5 select_reduce_fusion
  24.0 0.1 fusion.24
  24.2 50.0 %all-reduce.2.cloned.1.call-done = f32[128,1536]{1,0:T(8,128)} async-done(((f32[128,1536]{1,0:T(8,128)}), f32[128,1536]{1,0:T(8,128)}) %all-reduce.2.cloned.1.call-update) | async-done | bytes 786448 | tf_op jit(solution)/shard_map/psum | solution.py:40
  74.1 1.2 add_convert_fusion
  75.3 18.5 %scatter_custom_fusion = bf16[1280,1536]{1,0:T(8,128)(2,1)} fusion(s32[1024]{0:T(1024)S(1)} %bitcast.82, bf16[128,1536]{1,0:T(8,128)(2,1)S(1)} %add_convert_fusion, s32[1024]{0:T(1024)S(1)} %broadcast_clamp_fusion.1, bf16[]{:T(256)} %constant.68.clone.1), kind=kCustom, calls=%fused_computation.7 | custom fusion | bytes 3932162 | tf_op jit(solution)/shard_map/scatter | solution.py:48
  93.8 7.3 %reshape.252 = bf16[128,1,1,10,1536]{4,3,0,2,1:T(8,128)(2,1)} reshape(bf16[1280,1536]{1,0:T(8,128)(2,1)} %scatter_custom_fusion) | data formatting | bytes 7864320 | tf_op jit(solution)/shard_map/reshape | solution.py:49
  101.1 294.8 %all_to_all.8 = bf16[128,1,1,10,1536]{4,3,2,1,0:T(8,128)(2,1)S(1)} all-to-all(bf16[128,1,1,10,1536]{4,3,2,1,0:T(8,128)(2,1)} %bitcast.80), channel_id=1, replica_groups=mesh['ep'=128,'tp'=4] {'ep'}, dimensions={0} | all-to-all | bytes 7864320 | tf_op jit(solution)/shard_map/all_to_all | solution.py:52
  395.9 4.4 fusion.7
  400.3 0.9 fusion.15
  401.3 28.3 %all-gather.2.cloned.1.call-done = bf16[1,1,128,10,512]{4,2,3,1,0:T(8,128)(2,1)} async-done(((bf16[1,1,128,10,128]{4,2,3,1,0:T(8,128)(2,1)}), bf16[1,1,128,10,512]{4,2,3,1,0:T(8,128)(2,1)}) %all-gather.2.cloned.1.call-update) | async-done | bytes 1310736 | tf_op jit(solution)/shard_map/all_gather | solution.py:59
  429.6 2.2 fusion.10
  431.8 1.8 copy.65
  433.5 16.8 %all-to-all-start.1 = ((bf16[1,1,128,10,384]{4,3,0,1,2:T(8,128)(2,1)}), bf16[1,1,128,10,384]{4,3,0,1,2:T(8,128)(2,1)}, u32[]{:S(2)}, u32[]{:S(2)}) async-start(bf16[1,1,128,10,384]{4,3,0,1,2:T(8,128)(2,1)} %copy.65), calls=%async_computation.1 | async-start | bytes 3145728 | tf_op jit(solution)/shard_map/all_to_all | solution.py:64
  450.4 0.1 copy.54
  450.6 0.2 fusion.28
  450.8 7.1 %gather_fusion.1 = f32[1024]{0:T(1024)S(1)} fusion(f32[128,40]{0,1:T(8,128)S(1)} %fusion.28, s32[1024]{0:T(1024)S(1)} %reshape.275), kind=kCustom, calls=%fused_computation.2 | custom fusion | bytes 16384 | tf_op jit(solution)/shard_map/jit(take_along_axis)/gather | solution.py:43
  458.2 69.0 %all-to-all-done.1 = bf16[1,1,128,10,384]{4,3,0,1,2:T(8,128)(2,1)} async-done(((bf16[1,1,128,10,384]{4,3,0,1,2:T(8,128)(2,1)}), bf16[1,1,128,10,384]{4,3,0,1,2:T(8,128)(2,1)}, u32[]{:S(2)}, u32[]{:S(2)}) %all-to-all-start.1) | async-done | bytes 983072 | tf_op jit(solution)/shard_map/all_to_all | solution.py:64
  527.1 2.3 reshape.257
  529.4 3.9 gather_fusion
  533.4 0.5 fusion.6
  533.9 0.1 multiply_reduce_fusion
  534.0 9.8 %psum.15 = f32[128]{0:T(128)S(1)} all-reduce(f32[128]{0:T(128)S(1)} %multiply_reduce_fusion), channel_id=1, replica_groups=mesh['ep'=128,'tp'=4] {'tp'}, use_global_device_ids=true, to_apply=%region_13.14 | all-reduce | flops 128 | bytes 1024 | tf_op jit(solution)/shard_map/psum | solution.py:70
  543.8 0.7 multiply_convert_fusion
  (41 shorter events, 1.1 us)
Async XLA Ops:
  6.5 1.3 copy-start
  6.5 16.2 %copy-start.4 = (s32[128]{0:T(128)S(1)}, s32[128]{0:T(128)}, u32[]{:S(2)}) copy-start(s32[128]{0:T(128)} %param.14) | copy-start | bytes 1540
  6.5 67.6 %copy-start.1 = (bf16[128,1536]{1,0:T(8,128)(2,1)S(1)}, bf16[128,1536]{1,0:T(8,128)(2,1)}, u32[]{:S(2)}) copy-start(bf16[128,1536]{1,0:T(8,128)(2,1)} %param.10) | copy-start | bytes 1179652
  6.5 67.6 %all-reduce.2.cloned.1.call-start = ((), (), s32[]{:S(2)}) async-start(), calls=%async_computation.2 | async-start | bytes 1572864 | tf_op jit(solution)/shard_map/psum | solution.py:40
  10.0 419.6 %all-gather.2.cloned.1.call-start = ((), (), s32[]{:S(2)}) async-start(), calls=%async_computation.3 | async-start | bytes 1638400 | tf_op jit(solution)/shard_map/all_gather | solution.py:59
  101.1 294.8 %copy-start.6 = (bf16[1,1536,2,128]{3,2,1,0:T(2,128)(2,1)S(1)}, bf16[1,1536,2,128]{3,2,1,0:T(2,128)(2,1)}, u32[]{:S(2)}) copy-start(bf16[1,1536,2,128]{3,2,1,0:T(2,128)(2,1)} %param.15) | copy-start | bytes 2359300
  395.9 33.7 %copy-start.7 = (bf16[1,512,384]{2,1,0:T(8,128)(2,1)S(1)}, bf16[1,512,384]{2,1,0:T(8,128)(2,1)}, u32[]{:S(2)}) copy-start(bf16[1,512,384]{2,1,0:T(8,128)(2,1)} %param.16) | copy-start | bytes 1179652
  431.7 18.6 %copy-start.3 = (s32[128,8]{0,1:T(8,128)S(1)}, s32[128,8]{0,1:T(8,128)}, u32[]{:S(2)}) copy-start(s32[128,8]{0,1:T(8,128)} %param.13) | copy-start | bytes 12292
  431.7 18.8 %copy-start.2 = (bf16[1536,40]{0,1:T(8,128)(2,1)S(1)}, bf16[1536,40]{0,1:T(8,128)(2,1)}, u32[]{:S(2)}) copy-start(bf16[1536,40]{0,1:T(8,128)(2,1)} %param.12) | copy-start | bytes 368644
  433.5 93.6 %all-to-all-start.1 = ((bf16[1,1,128,10,384]{4,3,0,1,2:T(8,128)(2,1)}), bf16[1,1,128,10,384]{4,3,0,1,2:T(8,128)(2,1)}, u32[]{:S(2)}, u32[]{:S(2)}) async-start(bf16[1,1,128,10,384]{4,3,0,1,2:T(8,128)(2,1)} %copy.65), calls=%async_computation.1 | async-start | bytes 3145728 | tf_op jit(solution)/shard_map/all_to_all | solution.py:64
  529.4 14.4 %copy-start.5 = (f32[384]{0:T(512)S(1)}, f32[384]{0:T(512)}, u32[]{:S(2)}) copy-start(f32[384]{0:T(512)} %param.17) | copy-start | bytes 4612
Sparse Core Ops, SparseCore 0:
  10.1 63.9 all-reduce.1
  401.4 28.1 all-gather.1
where the time goes:
time: 552 us; the launch traced here: 551 us
  blocking collectives  305 us (55%)
  waiting for transfers between devices  147 us (27%)
  local copies, waits for them, and re-layouts  43.8 us (8%)
  starting transfers between devices  16.9 us (3%)
  other arithmetic  16.3 us (3%)
  between operations  13.7 us (2%)
  matrix products  8.91 us (2%)
    all_to_all x1, blocking collectives, per_device(): lax.all_to_all(send, 'ep', split_axis=0, concat_axis=2, tiled=True)  295 us
    all_to_all x1, waiting for transfers between devices, per_device(): back = lax.all_to_all(served, 'ep', split_axis=2, concat_axis=0, tiled=True)  69 us
    psum x1, waiting for transfers between devices, per_device(): proj = lax.psum(partial_value, 'tp')  50 us
    all_gather x1, waiting for transfers between devices, per_device(): lax.all_gather(hidden, 'tp', axis=4, tiled=True)  28.3 us
    scatter x1, local copies, waits for them, and re-layouts, per_device(): jnp.zeros((slots * capacity, width), jnp.bfloat16).at[dest]  18.5 us
    all_to_all x1, starting transfers between devices, per_device(): back = lax.all_to_all(served, 'ep', split_axis=2, concat_axis=0, tiled=True)  16.8 us
    another operation x3, other arithmetic  11.4 us
  transfers between devices with their start and end apart: 3, of which 3 were waited for; matrix products, arithmetic and copies ran while one was open for 4% of the time, Pallas kernels for 0%

commit v1 on v0

v1 whole, which is shorter than its diff:
```python
import jax
import jax.numpy as jnp
import numpy as np
from jax import lax
from jax.sharding import Mesh, PartitionSpec as P

E = 40
NZ, NX, NC, NY = 16, 4, 2, 4
NXC = NX * NC
ZS = NZ // NY
XCY = ("x", "c", "y")


def swap(x, axis):
    return lax.all_to_all(x, axis, 0, 0, tiled=True)


def sum_over_y(x):
    return jnp.sum(swap(jnp.broadcast_to(x[None], (NY,) + x.shape), "y"), axis=0)


def slot_tables(slot_expert, capacity):
    slots = slot_expert.shape[0]
    kinds = jnp.arange(E, dtype=jnp.int32)
    number = jnp.arange(slots, dtype=jnp.int32)
    same = slot_expert[:, None] == slot_expert[None, :]
    copies = jnp.sum(same.astype(jnp.int32), axis=1)
    copy_no = jnp.sum((same & (number[None, :] < number[:, None])).astype(jnp.int32), axis=1)
    hot = (slot_expert[:, None] == kinds[None, :]).astype(jnp.bfloat16)
    place = jnp.arange(capacity, dtype=jnp.int32)
    wanted = place[None, :] * copies[:, None] + copy_no[:, None]
    hot_q = jnp.broadcast_to(hot[:, None, :], (slots, capacity, E)).reshape(slots * capacity, E)
    return hot_q, wanted.reshape(slots * capacity)


def per_device(
    attn_out, residual, w_out, w_router, expert_ids, slot_expert, w_in, w_down, norm_gain
):
    rows, quarter = attn_out.shape
    width = residual.shape[1]
    topk = expert_ids.shape[1]
    slots = slot_expert.shape[0]
    capacity = (rows * topk * 5 // 4 + slots - 1) // slots
    total = slots * capacity
    per_z = NXC * capacity
    part = ZS * capacity
    served = NXC * part
    tp_pos = lax.axis_index("y")
    ff_part = w_in.shape[3]

    win_all = lax.all_gather(w_in.reshape(width, 2 * ff_part), "y")
    wdown_all = lax.all_gather(w_down[0], "y")

    partial_value = jnp.einsum(
        "rk,kqd->qrd", attn_out, w_out.reshape(quarter, NY, quarter),
        preferred_element_type=jnp.float32,
    )
    proj = jnp.sum(swap(partial_value, "y"), axis=0)
    mine = lax.dynamic_slice_in_dim(residual, tp_pos * quarter, quarter, 1)
    stream = (mine.astype(jnp.float32) + proj).astype(jnp.bfloat16)

    kinds = jnp.arange(E, dtype=jnp.int32)
    member = jnp.any(expert_ids[:, :, None] == kinds[None, None, :], axis=1)
    row_no = jnp.arange(rows, dtype=jnp.int32)
    earlier = (row_no[None, :] < row_no[:, None]).astype(jnp.bfloat16)
    rank = jnp.dot(earlier, member.astype(jnp.bfloat16), preferred_element_type=jnp.float32)
    rank = jnp.where(member, rank, -1.0).astype(jnp.bfloat16)
    hot_q, wanted = slot_tables(slot_expert, capacity)
    rank_q = lax.dot_general(
        hot_q, rank, (((1,), (1,)), ((), ())), preferred_element_type=jnp.float32
    )
    pick = rank_q == wanted.astype(jnp.float32)[:, None]
    send = jnp.dot(pick.astype(jnp.bfloat16), stream, preferred_element_type=jnp.float32)
    send = send.astype(jnp.bfloat16).reshape(NZ, per_z, quarter)
    came = swap(send, "z")
    came = came.reshape(NY, ZS, NXC, capacity, quarter).transpose(2, 0, 1, 3, 4)
    came = swap(came.reshape(NXC * NY, part, quarter), XCY)
    tokens = came.reshape(NXC, NY, part, quarter).transpose(0, 2, 1, 3).reshape(served, width)

    router_part = lax.dynamic_slice_in_dim(w_router, tp_pos * quarter, quarter, 0)
    logits = sum_over_y(jnp.dot(stream, router_part, preferred_element_type=jnp.float32))
    weights = jnp.where(member, jnp.exp(logits), 0.0)
    gates = weights / jnp.sum(weights, axis=1, keepdims=True)
    gates_hi = gates.astype(jnp.bfloat16)
    gates_lo = (gates - gates_hi.astype(jnp.float32)).astype(jnp.bfloat16)

    gu = jnp.einsum("rd,udc->urc", tokens, win_all, preferred_element_type=jnp.float32)
    hidden = (jax.nn.silu(gu[..., :ff_part]) * gu[..., ff_part:]).astype(jnp.bfloat16)
    hidden = hidden.transpose(1, 0, 2).reshape(served, NY * ff_part)
    outs = jnp.einsum("rf,tfd->trd", hidden, wdown_all, preferred_element_type=jnp.float32)
    outs = outs.astype(jnp.bfloat16).reshape(NY, NXC, part, quarter).transpose(1, 0, 2, 3)
    back = swap(outs.reshape(NXC * NY, part, quarter), XCY)
    back = back.reshape(NXC, NY, ZS, capacity, quarter).transpose(1, 2, 0, 3, 4)
    back = swap(back.reshape(NZ, per_z, quarter), "z").reshape(total, quarter)

    def weigh(part_of_gates):
        spread = lax.dot_general(
            hot_q, part_of_gates, (((1,), (1,)), ((), ())), preferred_element_type=jnp.float32
        )
        spread = jnp.where(pick, spread, 0.0).astype(jnp.bfloat16)
        return lax.dot_general(
            spread, back, (((0,), (0,)), ((), ())), preferred_element_type=jnp.float32
        )

    mixed = stream.astype(jnp.float32) + (weigh(gates_hi) + weigh(gates_lo))
    square = sum_over_y(jnp.sum(mixed * mixed, axis=1)[None, :])[0]
    scale = lax.rsqrt(square / width + 1e-06)
    return (mixed * scale[:, None] * norm_gain[None, :]).astype(jnp.bfloat16)


def solution(mesh):
    fine = Mesh(mesh.devices.reshape(NZ, NX, NC, NY), ("z", "x", "c", "y"))
    ep = ("z", "x", "c")
    return jax.shard_map(
        per_device,
        mesh=fine,
        in_specs=(
            P(ep, "y"),
            P(ep, None),
            P("y", None),
            P(),
            P(ep, None),
            P(),
            P(ep, None, None, "y"),
            P(ep, None, "y"),
            P("y"),
        ),
        out_specs=P(ep, "y"),
        check_vma=False,
    )
```

time: 552 us -> 223 us (0.40)
  blocking collectives: 305 us -> 29 us
  local copies, waits for them, and re-layouts: 43.8 us -> 10.6 us
  waiting for transfers between devices: 147 us -> 121 us
  starting transfers between devices: 16.9 us -> 36.1 us
  other arithmetic: 16.3 us -> 2.32 us
    all_to_all x1 -> x2, blocking collectives: 295 us -> 29 us  [swap(): return lax.all_to_all(x, axis, 0, 0, tiled=True)]
    all_to_all x1 -> x5, waiting for transfers between devices: 69 us -> 120 us  [swap(): return lax.all_to_all(x, axis, 0, 0, tiled=True)]
    psum x1 -> x0, waiting for transfers between devices: 50 us -> none  [per_device(): proj = lax.psum(partial_value, 'tp')]
    all_gather x1 -> x2, waiting for transfers between devices: 28.3 us -> 0.04 us  [the longest x1 0.02 us: per_device(): win_all = lax.all_gather(w_in.reshape(width, 2 * ff_part), 'y')]
    all_to_all x1 -> x5, starting transfers between devices: 16.8 us -> 36.1 us  [swap(): return lax.all_to_all(x, axis, 0, 0, tiled=True)]
    scatter x1 -> x0, local copies, waits for them, and re-layouts: 18.5 us -> none  [per_device(): jnp.zeros((slots * capacity, width), jnp.bfloat16).at[dest]]
    another operation x4 -> x0, other arithmetic: 11.6 us -> none
    gather x6 -> x0, local copies, waits for them, and re-layouts: 11.3 us -> none  [the longest x5 7.37 us: per_device(): picked = jnp.take_along_axis(logits, expert_ids, axis=1)]
  transfers between devices with their start and end apart: 3 -> 7, of which waited for: 3 -> 5; matrix products, arithmetic and copies ran while one was open for 4% -> 6% of each run, Pallas kernels for 0% -> 0%
where the time goes in v1:
time: 223 us; the launch traced here: 222 us
  waiting for transfers between devices  121 us (54%)
  starting transfers between devices  36.1 us (16%)
  blocking collectives  29 us (13%)
  between operations  13.7 us (6%)
  local copies, waits for them, and re-layouts  10.6 us (5%)
  matrix products  9.67 us (4%)
  other arithmetic  2.32 us (1%)
    all_to_all x5, waiting for transfers between devices, swap(): return lax.all_to_all(x, axis, 0, 0, tiled=True)  120 us
    all_to_all x5, starting transfers between devices, swap(): return lax.all_to_all(x, axis, 0, 0, tiled=True)  36.1 us
    all_to_all x2, blocking collectives, swap(): return lax.all_to_all(x, axis, 0, 0, tiled=True)  29 us
  transfers between devices with their start and end apart: 7, of which 5 were waited for; matrix products, arithmetic and copies ran while one was open for 6% of the time, Pallas kernels for 0%

profile of v1, /device:TPU:32, one launch (start us, length us, event | category | flops | bytes accessed | tf_op | source)
XLA Modules:
  0.0 222.0 jit_solution(2648512798567059317)
XLA Ops:
  6.5 3.2 %all_gather_reshape.3 = bf16[1,1536,256]{2,1,0:T(8,128)(2,1)} reshape(bf16[1,1536,2,128]{3,2,1,0:T(2,128)(2,1)} %param.15) | data formatting | bytes 1572864 | tf_op jit(solution)/shard_map/all_gather;reshape | solution.py:51
  9.8 0.7 copy.71
  10.7 1.4 convolution_bitcast_fusion.1
  12.0 4.6 %all-to-all-start = ((f32[4,128,384]{1,2,0:T(8,128)}), f32[4,128,384]{1,2,0:T(8,128)S(1)}, u32[]{:S(2)}, u32[]{:S(2)}) async-start(f32[4,128,384]{1,2,0:T(8,128)} %convolution_bitcast_fusion.1), calls=%async_computation | async-start | bytes 1572864 | tf_op jit(solution)/shard_map/all_to_all | solution.py:15
  17.4 0.4 convolution_compare_fusion
  17.9 11.0 %all-to-all-done = f32[4,128,384]{1,2,0:T(8,128)S(1)} async-done(((f32[4,128,384]{1,2,0:T(8,128)}), f32[4,128,384]{1,2,0:T(8,128)S(1)}, u32[]{:S(2)}, u32[]{:S(2)}) %all-to-all-start) | async-done | bytes 786464 | tf_op jit(solution)/shard_map/all_to_all | solution.py:15
  29.1 0.9 add_convert_fusion
  30.0 1.4 convolution_convert_fusion
  31.4 15.2 %all-to-all-start.2 = ((bf16[16,80,384]{2,1,0:T(8,128)(2,1)}), bf16[16,80,384]{2,1,0:T(8,128)(2,1)S(1)}, u32[]{:S(2)}, u32[]{:S(2)}) async-start(bf16[16,80,384]{2,1,0:T(8,128)(2,1)} %bitcast.3), calls=%async_computation.2 | async-start | bytes 1966080 | tf_op jit(solution)/shard_map/all_to_all | solution.py:15
  46.7 0.7 all-gather.5.cloned.1.call-update
  47.4 44.1 %all-to-all-done.2 = bf16[16,80,384]{2,1,0:T(8,128)(2,1)S(1)} async-done(((bf16[16,80,384]{2,1,0:T(8,128)(2,1)}), bf16[16,80,384]{2,1,0:T(8,128)(2,1)S(1)}, u32[]{:S(2)}, u32[]{:S(2)}) %all-to-all-start.2) | async-done | bytes 983072 | tf_op jit(solution)/shard_map/all_to_all | solution.py:15
  91.9 0.4 copy.72
  92.3 0.4 reshape.112
  92.7 21.4 %all_to_all.35 = bf16[32,40,384]{2,1,0:T(8,128)(2,1)S(1)} all-to-all(bf16[32,40,384]{2,1,0:T(8,128)(2,1)S(1)} %reshape.112), channel_id=1, replica_groups=mesh['z'=16,'x'=4,'c'=2,'y'=4] {'x','c','y'}, dimensions={0} | all-to-all | bytes 1966080 | tf_op jit(solution)/shard_map/all_to_all | solution.py:15
  114.1 0.4 copy.64
  114.5 0.4 reshape.110
  114.9 3.1 %convolution_bitcast_fusion = f32[4,320,256]{2,1,0:T(8,128)S(1)} fusion(bf16[320,1536,1]{1,0,2:T(8,128)(2,1)S(1)} %reshape.110, bf16[4,1536,256]{2,1,0:T(8,128)(2,1)} %all-gather.3.cloned.1.call-done), kind=kOutput, calls=%fused_computation.7 | convolution fusion | flops 1006632960 | bytes 5439488 | tf_op jit(solution)/shard_map/rd,udc->urc/dot_general | solution.py:87
  118.6 2.1 convolution_convert_fusion.1
  120.7 1.1 copy.66
  121.7 3.9 %all-to-all-start.4 = ((bf16[32,40,384]{2,1,0:T(8,128)(2,1)}), bf16[32,40,384]{2,1,0:T(8,128)(2,1)S(1)}, u32[]{:S(2)}, u32[]{:S(2)}) async-start(bf16[32,40,384]{2,1,0:T(8,128)(2,1)} %bitcast.12), calls=%async_computation.4 | async-start | bytes 1966080 | tf_op jit(solution)/shard_map/all_to_all | solution.py:15
  125.8 16.2 %all-to-all-done.4 = bf16[32,40,384]{2,1,0:T(8,128)(2,1)S(1)} async-done(((bf16[32,40,384]{2,1,0:T(8,128)(2,1)}), bf16[32,40,384]{2,1,0:T(8,128)(2,1)S(1)}, u32[]{:S(2)}, u32[]{:S(2)}) %all-to-all-start.4) | async-done | bytes 983072 | tf_op jit(solution)/shard_map/all_to_all | solution.py:15
  142.0 0.6 broadcast_in_dim.19
  142.6 3.3 %all-to-all-start.1 = ((f32[4,128,40]{1,2,0:T(8,128)}), f32[4,128,40]{1,2,0:T(8,128)S(1)}, u32[]{:S(2)}, u32[]{:S(2)}) async-start(f32[4,128,40]{1,2,0:T(8,128)} %broadcast_in_dim.19), calls=%async_computation.1 | async-start | bytes 163840 | tf_op jit(solution)/shard_map/all_to_all | solution.py:15
  146.3 0.4 copy.73
  146.8 1.2 reshape.115
  147.9 3.7 %all-to-all-done.1 = f32[4,128,40]{1,2,0:T(8,128)S(1)} async-done(((f32[4,128,40]{1,2,0:T(8,128)}), f32[4,128,40]{1,2,0:T(8,128)S(1)}, u32[]{:S(2)}, u32[]{:S(2)}) %all-to-all-start.1) | async-done | bytes 81952 | tf_op jit(solution)/shard_map/all_to_all | solution.py:15
  151.6 9.0 %all-to-all-start.5 = ((bf16[16,80,384]{2,1,0:T(8,128)(2,1)}), bf16[16,80,384]{2,1,0:T(8,128)(2,1)S(1)}, u32[]{:S(2)}, u32[]{:S(2)}) async-start(bf16[16,80,384]{2,1,0:T(8,128)(2,1)} %reshape.115), calls=%async_computation.5 | async-start | bytes 1966080 | tf_op jit(solution)/shard_map/all_to_all | solution.py:15
  160.7 44.8 %all-to-all-done.5 = bf16[16,80,384]{2,1,0:T(8,128)(2,1)S(1)} async-done(((bf16[16,80,384]{2,1,0:T(8,128)(2,1)}), bf16[16,80,384]{2,1,0:T(8,128)(2,1)S(1)}, u32[]{:S(2)}, u32[]{:S(2)}) %all-to-all-start.5) | async-done | bytes 983072 | tf_op jit(solution)/shard_map/all_to_all | solution.py:15
  205.5 0.6 fusion.2
  206.1 0.7 multiply_reduce_fusion
  206.8 7.6 %all_to_all.36 = f32[4,1,128]{2,1,0:T(1,128)S(1)} all-to-all(f32[4,1,128]{2,1,0:T(1,128)S(1)} %broadcast_in_dim.22), channel_id=1, replica_groups=mesh['z'=16,'x'=4,'c'=2,'y'=4] {'y'}, dimensions={0} | all-to-all | bytes 4096 | tf_op jit(solution)/shard_map/all_to_all | solution.py:15
  214.4 0.7 multiply_convert_fusion
  (39 shorter events, 2.7 us)
Async XLA Ops:
  6.5 119.1 %copy-start = (bf16[1536,40]{0,1:T(8,128)(2,1)S(1)}, bf16[1536,40]{0,1:T(8,128)(2,1)}, u32[]{:S(2)}) copy-start(bf16[1536,40]{0,1:T(8,128)(2,1)} %param.12) | copy-start | bytes 368644
  6.5 3.3 %copy-start.1 = (bf16[384,1536]{1,0:T(8,128)(2,1)S(1)}, bf16[384,1536]{1,0:T(8,128)(2,1)}, u32[]{:S(2)}) copy-start(bf16[384,1536]{1,0:T(8,128)(2,1)} %param.11) | copy-start | bytes 3538948
  6.5 108.4 %all-gather.3.cloned.1.call-start = ((), (), s32[]{:S(2)}) async-start(), calls=%async_computation.7 | async-start | bytes 3932160 | tf_op jit(solution)/shard_map/all_gather | solution.py:51
  9.8 0.9 copy-start.2
  10.7 5.9 %copy-start.3 = (s32[128]{0:T(128)S(1)}, s32[128]{0:T(128)}, u32[]{:S(2)}) copy-start(s32[128]{0:T(128)} %param.14) | copy-start | bytes 1540
  12.0 5.4 %copy-start.4 = (s32[128,8]{0,1:T(8,128)S(1)}, s32[128,8]{0,1:T(8,128)}, u32[]{:S(2)}) copy-start(s32[128,8]{0,1:T(8,128)} %param.13) | copy-start | bytes 12292
  12.0 16.9 %all-to-all-start = ((f32[4,128,384]{1,2,0:T(8,128)}), f32[4,128,384]{1,2,0:T(8,128)S(1)}, u32[]{:S(2)}, u32[]{:S(2)}) async-start(f32[4,128,384]{1,2,0:T(8,128)} %convolution_bitcast_fusion.1), calls=%async_computation | async-start | bytes 1572864 | tf_op jit(solution)/shard_map/all_to_all | solution.py:15
  31.4 60.1 %all-to-all-start.2 = ((bf16[16,80,384]{2,1,0:T(8,128)(2,1)}), bf16[16,80,384]{2,1,0:T(8,128)(2,1)S(1)}, u32[]{:S(2)}, u32[]{:S(2)}) async-start(bf16[16,80,384]{2,1,0:T(8,128)(2,1)} %bitcast.3), calls=%async_computation.2 | async-start | bytes 1966080 | tf_op jit(solution)/shard_map/all_to_all | solution.py:15
  46.6 72.0 %all-gather.5.cloned.1.call-start = ((), (), s32[]{:S(2)}) async-start(), calls=%async_computation.8 | async-start | bytes 1966080 | tf_op jit(solution)/shard_map/all_gather | solution.py:52
  121.7 20.3 %all-to-all-start.4 = ((bf16[32,40,384]{2,1,0:T(8,128)(2,1)}), bf16[32,40,384]{2,1,0:T(8,128)(2,1)S(1)}, u32[]{:S(2)}, u32[]{:S(2)}) async-start(bf16[32,40,384]{2,1,0:T(8,128)(2,1)} %bitcast.12), calls=%async_computation.4 | async-start | bytes 1966080 | tf_op jit(solution)/shard_map/all_to_all | solution.py:15
  142.6 9.0 %all-to-all-start.1 = ((f32[4,128,40]{1,2,0:T(8,128)}), f32[4,128,40]{1,2,0:T(8,128)S(1)}, u32[]{:S(2)}, u32[]{:S(2)}) async-start(f32[4,128,40]{1,2,0:T(8,128)} %broadcast_in_dim.19), calls=%async_computation.1 | async-start | bytes 163840 | tf_op jit(solution)/shard_map/all_to_all | solution.py:15
  151.6 53.9 %all-to-all-start.5 = ((bf16[16,80,384]{2,1,0:T(8,128)(2,1)}), bf16[16,80,384]{2,1,0:T(8,128)(2,1)S(1)}, u32[]{:S(2)}, u32[]{:S(2)}) async-start(bf16[16,80,384]{2,1,0:T(8,128)(2,1)} %reshape.115), calls=%async_computation.5 | async-start | bytes 1966080 | tf_op jit(solution)/shard_map/all_to_all | solution.py:15
  205.5 8.9 %copy-start.5 = (f32[384]{0:T(512)S(1)}, f32[384]{0:T(512)}, u32[]{:S(2)}) copy-start(f32[384]{0:T(512)} %param.17) | copy-start | bytes 4612
Sparse Core Ops, SparseCore 0:
  9.9 51.2 all-gather.2
  63.3 34.3 all-gather.4
